TPU v7x, 32 devices: a whole 2x2x4 slice. The times are simulated.
32 devices in a mesh: groups: 2 (over x), seq: 16 (over z, y, core).
Axes of the slice: x: 2, y: 2, z: 4, core: 2. Of those that a mesh axis runs over, the one named last changes fastest.
Arguments:
- window_queries: bfloat16 [4096, 2048], P(('groups', 'seq')), parts along dimension 0, may hold values from -300 to 300
- window_kv: bfloat16 [4096, 512], P(('groups', 'seq')), parts along dimension 0, may hold values from -6 to 6
- stream: bfloat16 [4096, 2880], P(('groups', 'seq')), parts along dimension 0, may hold values from -6 to 6
- moe_gain: float32 [2880], replicated, may hold values from 0.25 to 1.75
- routes: int32 [4096, 4], P(('groups', 'seq')), parts along dimension 0, may hold values from 0 to 15, as said below
- route_gates: float32 [4096, 4], P(('groups', 'seq')), parts along dimension 0, may hold values from 0.1 to 0.6
- gate_proj: bfloat16 [2880, 23040], P(None, 'seq'), may hold values from -0.109375 to 0.109375
- up_proj: bfloat16 [2880, 23040], P(None, 'seq'), may hold values from -0.109375 to 0.109375
- down_proj: bfloat16 [23040, 2880], P('seq'), may hold values from -0.15625 to 0.15625
- attn_gain: float32 [2880], replicated, may hold values from 0.25 to 1.75
- kv_proj: bfloat16 [2880, 512], replicated, may hold values from -0.109375 to 0.109375
- tract_queries: bfloat16 [4096, 2048], P(('groups', 'seq')), parts along dimension 0, may hold values from -300 to 300
Outputs:
- attn_window: bfloat16 [4096, 2048], P(('groups', 'seq')), parts along dimension 0
- stream_next: bfloat16 [4096, 2880], P(('groups', 'seq')), parts along dimension 0
- attn_tract: bfloat16 [4096, 2048], P(('groups', 'seq')), parts along dimension 0
There are 2 independent parts, one for each index of `groups`. A program takes and returns all parts, laid end to end along the dimension named above; an argument that names none is the same for every part. Nothing has to cross between parts.
Inputs may be any that keep to these rules, and one draw needn't show every extreme that they name: `routes`: in each device's block of 128 tokens every expert is named exactly 32 times; a token names 4 different experts.
All inputs are finite; a program needn't handle non-finite values.
Results may differ from a plain program's by a relative error of at most 0.025.
The roundings to bfloat16 on the way count: a program that leaves them out, or rounds other values in their place, can miss the bound.
Values may be sent and summed in bfloat16 or wider, within the bound.
No kernel may reach another device: no remote copies, remote signals or barrier semaphores. Data moves between devices by JAX's collectives and lax.ppermute only.
A program may use at most 128 MiB of HBM per device.

v0:
```python
import jax
import jax.numpy as jnp
from jax import lax
from jax.sharding import PartitionSpec as P

HEADS = 32
KV_HEADS = 4
HEAD_DIM = 64
EXPERTS = 16
TOP = 4
WINDOW = 128
STRETCH = 1024


def from_behind(block, axis, distance):
    devices = range(lax.axis_size(axis))
    route = [(i - distance, i) for i in devices if i - distance in devices]
    return lax.ppermute(block, axis, route)


def normed(values, gain):
    widened = values.astype(jnp.float32)
    second = jnp.mean(widened * widened, axis=-1, keepdims=True)
    return (widened * lax.rsqrt(second + 1e-05) * gain).astype(jnp.bfloat16)


def attend(queries, keys, values, allowed):
    query_rows = queries.shape[0]
    key_rows = keys.shape[0]
    group_size = HEADS // KV_HEADS
    query_heads = queries.reshape(query_rows, KV_HEADS, group_size, HEAD_DIM)
    key_heads = keys.reshape(key_rows, KV_HEADS, HEAD_DIM)
    value_heads = values.reshape(key_rows, KV_HEADS, HEAD_DIM)
    scores = (
        jnp.einsum("qkgd,skd->kgqs", query_heads, key_heads, preferred_element_type=jnp.float32)
        * 0.125
    )
    scores = jnp.where(allowed, scores, -1e30)
    peak = jnp.max(scores, axis=-1, keepdims=True)
    weights = jnp.exp(scores - peak)
    totals = jnp.sum(weights, axis=-1)
    mixed = jnp.einsum(
        "kgqs,skd->qkgd",
        weights.astype(jnp.bfloat16),
        value_heads,
        preferred_element_type=jnp.float32,
    )
    mixed = mixed / jnp.transpose(totals, (2, 0, 1))[..., None]
    return mixed.reshape(query_rows, HEADS * HEAD_DIM).astype(jnp.bfloat16)


def on_device(
    window_queries,
    window_kv,
    stream,
    moe_gain,
    routes,
    route_gates,
    gate_proj,
    up_proj,
    down_proj,
    attn_gain,
    kv_proj,
    tract_queries,
):
    rows_here = window_queries.shape[0]
    half_cols = window_kv.shape[1] // 2
    device = lax.axis_index("seq")
    devices = lax.axis_size("seq")
    query_block = min(512, rows_here)
    first_row = device * rows_here
    rim_keys = from_behind(window_kv, "seq", 1)
    window_keys = jnp.concatenate([rim_keys, window_kv], 0)
    offset = 0
    query_pos = first_row + offset + jnp.arange(query_block, dtype=jnp.int32)
    key_pos = first_row + offset - WINDOW + jnp.arange(query_block + WINDOW, dtype=jnp.int32)
    distance = query_pos[:, None] - key_pos[None, :]
    allowed = (distance >= 0) & (distance < WINDOW) & (key_pos[None, :] >= 0)
    window_parts = attend(
        window_queries, window_keys[:, :half_cols], window_keys[:, half_cols:], allowed
    )
    moe_input = normed(stream, moe_gain)
    model_width = moe_input.shape[1]
    capacity = rows_here * TOP // EXPERTS
    split_count = devices // EXPERTS
    flat_routes = routes.reshape(-1)
    onehot = (flat_routes[:, None] == jnp.arange(EXPERTS, dtype=jnp.int32)[None, :]).astype(
        jnp.int32
    )
    slot_rank = jnp.sum(onehot * (jnp.cumsum(onehot, axis=0) - 1), axis=1)
    slot_index = flat_routes * capacity + slot_rank
    token_ids = jnp.arange(rows_here * TOP, dtype=jnp.int32) // TOP
    slot_table = jnp.zeros((EXPERTS * capacity,), jnp.int32).at[slot_index].set(token_ids)
    outgoing = moe_input[slot_table].reshape(EXPERTS, capacity, model_width)
    copies = jnp.repeat(outgoing, split_count, axis=0)
    arrived = lax.all_to_all(copies, "seq", split_axis=0, concat_axis=0, tiled=True)
    flat_rows = arrived.reshape(-1, model_width)
    gate_vals = jnp.dot(flat_rows, gate_proj, preferred_element_type=jnp.float32)
    up_vals = jnp.dot(flat_rows, up_proj, preferred_element_type=jnp.float32)
    hidden = (jax.nn.silu(gate_vals) * up_vals).astype(jnp.bfloat16)
    block_out = jnp.dot(hidden, down_proj, preferred_element_type=jnp.float32).astype(jnp.bfloat16)
    partial_value = block_out.reshape(arrived.shape)
    returned = lax.all_to_all(partial_value, "seq", split_axis=0, concat_axis=0, tiled=True)
    summed = jnp.sum(
        returned.astype(jnp.float32).reshape(EXPERTS, split_count, capacity, model_width), axis=1
    )
    summed = summed.reshape(EXPERTS * capacity, model_width)
    picked = summed[slot_index].reshape(rows_here, TOP, model_width)
    stream_next = (
        stream.astype(jnp.float32) + jnp.sum(picked * route_gates[:, :, None], axis=1)
    ).astype(jnp.bfloat16)
    attn_input = normed(stream_next, attn_gain)
    tract_kv = jnp.dot(attn_input, kv_proj, preferred_element_type=jnp.float32).astype(jnp.bfloat16)
    lead = STRETCH // 2
    back_devices = STRETCH // rows_here - 1
    earlier = []
    for shift_by in range(back_devices, 0, -1):
        earlier.append(from_behind(tract_kv, "seq", shift_by))
    context_keys = jnp.concatenate(earlier + [tract_kv], 0)
    key_pos = (
        first_row
        - back_devices * rows_here
        + jnp.arange((back_devices + 1) * rows_here, dtype=jnp.int32)
    )
    offset = 0
    query_pos = first_row + offset + jnp.arange(query_block, dtype=jnp.int32)
    allowed = (
        (key_pos[None, :] <= query_pos[:, None])
        & (key_pos[None, :] >= 0)
        & ((key_pos[None, :] + lead) // STRETCH == (query_pos[:, None] + lead) // STRETCH)
    )
    tract_parts = attend(
        tract_queries, context_keys[:, :half_cols], context_keys[:, half_cols:], allowed
    )
    return (window_parts, stream_next, tract_parts)


def solution(mesh):
    return jax.shard_map(
        on_device,
        mesh=mesh,
        in_specs=(
            P(("groups", "seq"), None),
            P(("groups", "seq"), None),
            P(("groups", "seq"), None),
            P(),
            P(("groups", "seq"), None),
            P(("groups", "seq"), None),
            P(None, "seq"),
            P(None, "seq"),
            P("seq", None),
            P(),
            P(),
            P(("groups", "seq"), None),
        ),
        out_specs=(
            P(("groups", "seq"), None),
            P(("groups", "seq"), None),
            P(("groups", "seq"), None),
        ),
        check_vma=False,
    )
```

profile of v0, /device:TPU:0, one launch (start us, length us, event | category | flops | bytes accessed | tf_op | source)
XLA Modules:
  0.0 309.0 jit_solution(2998349848496716185)
XLA Ops:
  4.2 2.4 scatter_custom_fusion
  6.7 2.3 copy.33
  10.4 2.2 fusion.18
  12.6 7.9 %gather_fusion = bf16[512,2880]{1,0:T(8,128)(2,1)} fusion(bf16[128,2880]{1,0:T(8,128)(2,1)} %fusion.18, s32[1024]{0:T(1024)S(1)} %pad_clamp_fusion.1), kind=kCustom, calls=%fused_computation | custom fusion | bytes 5900288 | tf_op jit(solution)/shard_map/gather | solution.py:94
  20.5 74.9 %all_to_all.10 = bf16[16,32,2880]{2,1,0:T(8,128)(2,1)S(1)} all-to-all(bf16[16,32,2880]{2,1,0:T(8,128)(2,1)} %bitcast.96), channel_id=1, replica_groups=mesh['groups'=2,'seq'=16] {'seq'}, dimensions={0} | all-to-all | bytes 5898240 | tf_op jit(solution)/shard_map/all_to_all | solution.py:96
  97.1 9.0 %fusion.54 = f32[512,1440]{0,1:T(8,128)} fusion(bf16[512,2880]{1,0:T(8,128)(2,1)S(1)} %bitcast.97, bf16[2880,1440]{0,1:T(8,128)(2,1)} %param.18), kind=kOutput, calls=%fused_computation.103 | convolution fusion | flops 4246732800 | bytes 14192640 | tf_op jit(solution)/shard_map/dot_general | solution.py:98
  106.1 26.3 %convolution_convert_fusion = bf16[512,2880]{0,1:T(8,128)(2,1)} fusion(bf16[1440,2880]{1,0:T(8,128)(2,1)} %param.20, bf16[512,2880]{1,0:T(8,128)(2,1)} %bitcast.98, bf16[2880,1440]{0,1:T(8,128)(2,1)} %param.19, f32[512,1440]{0,1:T(8,128)} %fusion.54), kind=kOutput, calls=%fused_computation.11 | convolution fusion | flops 8499363840 | bytes 25436160 | tf_op jit(solution)/shard_map/dot_general | solution.py:101
  132.3 4.6 %copy.38 = bf16[512,2880]{1,0:T(8,128)(2,1)} copy(bf16[512,2880]{0,1:T(8,128)(2,1)} %convolution_convert_fusion) | data formatting | bytes 5898240 | tf_op jit(solution)/shard_map/convert_element_type | solution.py:101
  137.0 4.9 %all-to-all-start.1 = ((bf16[16,32,2880]{2,1,0:T(8,128)(2,1)}), bf16[16,32,2880]{2,1,0:T(8,128)(2,1)}, u32[]{:S(2)}, u32[]{:S(2)}) async-start(bf16[16,32,2880]{2,1,0:T(8,128)(2,1)} %bitcast.95), calls=%async_computation.1 | async-start | bytes 6029312 | tf_op jit(solution)/shard_map/all_to_all | solution.py:103
  141.8 2.7 collective-permute-start
  146.4 2.0 copy.42
  155.5 43.3 %all-to-all-done.1 = bf16[16,32,2880]{2,1,0:T(8,128)(2,1)} async-done(((bf16[16,32,2880]{2,1,0:T(8,128)(2,1)}), bf16[16,32,2880]{2,1,0:T(8,128)(2,1)}, u32[]{:S(2)}, u32[]{:S(2)}) %all-to-all-start.1) | async-done | bytes 2949152 | tf_op jit(solution)/shard_map/all_to_all | solution.py:103
  198.8 4.8 %bitcast_convert_fusion = f32[512,2880]{1,0:T(8,128)} fusion(bf16[16,32,2880]{2,1,0:T(8,128)(2,1)} %all-to-all-done.1), kind=kLoop, calls=%fused_computation.18 | loop fusion | flops 1474560 | bytes 8847360 | tf_op jit(solution)/shard_map/reshape | solution.py:107
  203.7 9.7 %gather_fusion.1 = f32[512,2880]{1,0:T(8,128)} fusion(f32[512,2880]{1,0:T(8,128)} %bitcast_convert_fusion, s32[1024]{0:T(1024)S(1)} %pad_clamp_fusion), kind=kCustom, calls=%fused_computation.1 | custom fusion | bytes 11798528 | tf_op jit(solution)/shard_map/gather | solution.py:108
  213.3 7.7 %reshape.220 = f32[128,4,2880]{2,1,0:T(4,128)} reshape(f32[512,2880]{1,0:T(8,128)} %gather_fusion.1) | data formatting | bytes 11796480 | tf_op jit(solution)/shard_map/reshape | solution.py:108
  221.0 7.2 %multiply_reduce_fusion = f32[128,2880]{1,0:T(8,128)S(1)} fusion(f32[128,4,2880]{2,1,0:T(4,128)} %reshape.220, f32[128,4]{1,0:T(8,128)S(1)} %copy-done.7), kind=kLoop, calls=%fused_computation.10 | loop fusion | flops 2580480 | bytes 7374848 | tf_op jit(solution)/shard_map/reduce_sum | solution.py:110
  230.1 19.8 %collective-permute-start.1 = (bf16[128,512]{1,0:T(8,128)(2,1)S(1)}, bf16[128,512]{1,0:T(8,128)(2,1)}, u32[]{:S(2)}, u32[]{:S(2)}) collective-permute-start(bf16[128,512]{1,0:T(8,128)(2,1)S(1)} %convolution_convert_fusion.1), channel_id=1, source_target_pairs={{0,7},{1,8},{2,9},{3,10},{4,11},{5,12},{6,13},{7,14},{8,15},{16,23... | collective-permute-start | bytes 393224 | tf_op jit(solution)/shard_map/ppermute | solution.py:18
  253.3 2.0 copy.44
  259.2 5.9 %collective-permute-start.5 = (bf16[128,512]{1,0:T(8,128)(2,1)S(1)}, bf16[128,512]{1,0:T(8,128)(2,1)S(1)}, u32[]{:S(2)}, u32[]{:S(2)}) collective-permute-start(bf16[128,512]{1,0:T(8,128)(2,1)S(1)} %convolution_convert_fusion.1), channel_id=1, source_target_pairs={{0,3},{1,4},{2,5},{3,6},{4,7},{5,8},{6,9},{7,10},{8,11},{9,12},{10... | collective-permute-start | bytes 393224 | tf_op jit(solution)/shard_map/ppermute | solution.py:18
  265.1 2.3 copy.45
  269.6 2.6 collective-permute-start.7
  279.3 9.3 %fusion.2 = (f32[4,8,128]{2,1,0:T(8,128)S(1)}, f32[4,1024,128,8]{2,1,3,0:T(8,128)}) fusion(pred[128,1024]{0,1:T(8,128)(4,1)S(1)} %compare_and_fusion, bf16[1024,4,64,1]{0,2,3,1:T(8,128)(2,1)} %bitcast.101, bf16[128,4,8,64]{0,3,2,1:T(8,128)(2,1)} %bitcast.99), kind=kOutput, calls=%fused_computation.7 | convolution fusion | flops 549449728 | bytes 17973248 | tf_op jit(solution)/shard_map/qkgd,skd->kgqs/dot_general | solution.py:35
  288.6 9.4 %fusion = f32[4,8,128]{2,1,0:T(8,128)S(1)} fusion(f32[4,1024,128,8]{2,1,3,0:T(8,128)} %get-tuple-element.18, f32[4,8,128]{2,1,0:T(8,128)S(1)} %get-tuple-element.17, pred[128,1024]{0,1:T(8,128)(4,1)S(1)} %compare_and_fusion), kind=kLoop, calls=%fused_computation.5 | loop fusion | flops 16773120 | bytes 16941056 | tf_op jit(solution)/shard_map/reduce_sum | solution.py:41
  298.0 8.6 %divide_convert_fusion = bf16[128,4,8,64]{0,3,2,1:T(8,128)(2,1)} fusion(bf16[1024,4,64,1]{0,2,3,1:T(8,128)(2,1)S(1)} %bitcast.103, f32[4,1024,128,8]{2,1,3,0:T(8,128)} %get-tuple-element.18, f32[4,8,128]{2,1,0:T(8,128)S(1)} %get-tuple-element.17, pred[128,1024]{0,1:T(8,128)(4,1)S(1)} %compare_and_fusion, f32[128,4,8]{0,2,1:T(8,128)S(1)} %bitcast.108), kind=kOutput, calls=%fused_computation.37 | convolution fusion | flops 554172416 | bytes 17989632 | tf_op jit(solution)/shard_map/kgqs,skd->qkgd/dot_general | solution.py:42
  (85 shorter events, 35.7 us)
Async XLA Ops:
  0.6 228.8 %copy-start = (bf16[2880,512]{1,0:T(8,128)(2,1)S(1)}, bf16[2880,512]{1,0:T(8,128)(2,1)}, u32[]{:S(2)}) copy-start(bf16[2880,512]{1,0:T(8,128)(2,1)} %param.22) | copy-start | bytes 8847364
  95.5 1.6 copy-start.4
  137.0 4.9 %copy-start.8 = (bf16[128,512]{1,0:T(8,128)(2,1)S(1)}, bf16[128,512]{1,0:T(8,128)(2,1)}, u32[]{:S(2)}) copy-start(bf16[128,512]{1,0:T(8,128)(2,1)} %param.13) | copy-start | bytes 393220
  137.0 8.7 %copy-start.9 = (f32[128,4]{0,1:T(4,128)S(1)}, f32[128,4]{0,1:T(4,128)}, u32[]{:S(2)}) copy-start(f32[128,4]{0,1:T(4,128)} %param.17) | copy-start | bytes 6148
  137.0 61.9 %all-to-all-start.1 = ((bf16[16,32,2880]{2,1,0:T(8,128)(2,1)}), bf16[16,32,2880]{2,1,0:T(8,128)(2,1)}, u32[]{:S(2)}, u32[]{:S(2)}) async-start(bf16[16,32,2880]{2,1,0:T(8,128)(2,1)} %bitcast.95), calls=%async_computation.1 | async-start | bytes 6029312 | tf_op jit(solution)/shard_map/all_to_all | solution.py:103
  141.8 8.7 %collective-permute-start = (bf16[128,512]{1,0:T(8,128)(2,1)S(1)}, bf16[128,512]{1,0:T(8,128)(2,1)S(1)}, u32[]{:S(2)}, u32[]{:S(2)}) collective-permute-start(bf16[128,512]{1,0:T(8,128)(2,1)S(1)} %copy-done.8), channel_id=1, source_target_pairs={{0,1},{1,2},{2,3},{3,4},{4,5},{5,6},{6,7},{7,8},{8,9},{9,10},{10,1... | collective-permute-start | bytes 393224 | tf_op jit(solution)/shard_map/ppermute | solution.py:18
  152.6 2.0 copy-start.1
  213.3 7.7 %copy-start.7 = (f32[128,4]{1,0:T(8,128)S(1)}, f32[128,4]{1,0:T(8,128)}, u32[]{:S(2)}) copy-start(f32[128,4]{1,0:T(8,128)} %copy.39) | copy-start | bytes 6148
  221.0 7.2 %copy-start.3 = (bf16[128,2880]{1,0:T(8,128)(2,1)S(1)}, bf16[128,2880]{1,0:T(8,128)(2,1)}, u32[]{:S(2)}) copy-start(bf16[128,2880]{1,0:T(8,128)(2,1)} %copy.33) | copy-start | bytes 2211844
  221.0 8.4 %copy-start.10 = (f32[2880]{0:T(1024)S(1)}, f32[2880]{0:T(1024)}, u32[]{:S(2)}) copy-start(f32[2880]{0:T(1024)} %param.21) | copy-start | bytes 34564
  228.2 23.2 %copy-start.2 = (f32[4,256,128,8]{2,1,3,0:T(8,128)S(1)}, f32[4,256,128,8]{2,1,3,0:T(8,128)}, u32[]{:S(2)}) copy-start(f32[4,256,128,8]{2,1,3,0:T(8,128)} %copy-done.1) | copy-start | bytes 12582916
  228.5 0.9 copy-start.5
  230.1 37.3 %collective-permute-start.1 = (bf16[128,512]{1,0:T(8,128)(2,1)S(1)}, bf16[128,512]{1,0:T(8,128)(2,1)}, u32[]{:S(2)}, u32[]{:S(2)}) collective-permute-start(bf16[128,512]{1,0:T(8,128)(2,1)S(1)} %convolution_convert_fusion.1), channel_id=1, source_target_pairs={{0,7},{1,8},{2,9},{3,10},{4,11},{5,12},{6,13},{7,14},{8,15},{16,23... | collective-permute-start | bytes 393224 | tf_op jit(solution)/shard_map/ppermute | solution.py:18
  249.8 19.7 %collective-permute-start.2 = (bf16[128,512]{1,0:T(8,128)(2,1)S(1)}, bf16[128,512]{1,0:T(8,128)(2,1)S(1)}, u32[]{:S(2)}, u32[]{:S(2)}) collective-permute-start(bf16[128,512]{1,0:T(8,128)(2,1)S(1)} %convolution_convert_fusion.1), channel_id=1, source_target_pairs={{0,6},{1,7},{2,8},{3,9},{4,10},{5,11},{6,12},{7,13},{8,14},{9,15},... | collective-permute-start | bytes 393224 | tf_op jit(solution)/shard_map/ppermute | solution.py:18
  255.3 16.9 %collective-permute-start.3 = (bf16[128,512]{1,0:T(8,128)(2,1)S(1)}, bf16[128,512]{1,0:T(8,128)(2,1)}, u32[]{:S(2)}, u32[]{:S(2)}) collective-permute-start(bf16[128,512]{1,0:T(8,128)(2,1)S(1)} %convolution_convert_fusion.1), channel_id=1, source_target_pairs={{0,5},{1,6},{2,7},{3,8},{4,9},{5,10},{6,11},{7,12},{8,13},{9,14},{... | collective-permute-start | bytes 393224 | tf_op jit(solution)/shard_map/ppermute | solution.py:18
  257.2 15.9 %collective-permute-start.4 = (bf16[128,512]{1,0:T(8,128)(2,1)S(1)}, bf16[128,512]{1,0:T(8,128)(2,1)}, u32[]{:S(2)}, u32[]{:S(2)}) collective-permute-start(bf16[128,512]{1,0:T(8,128)(2,1)S(1)} %convolution_convert_fusion.1), channel_id=1, source_target_pairs={{0,4},{1,5},{2,6},{3,7},{4,8},{5,9},{6,10},{7,11},{8,12},{9,13},{1... | collective-permute-start | bytes 393224 | tf_op jit(solution)/shard_map/ppermute | solution.py:18
  259.2 14.9 %collective-permute-start.5 = (bf16[128,512]{1,0:T(8,128)(2,1)S(1)}, bf16[128,512]{1,0:T(8,128)(2,1)S(1)}, u32[]{:S(2)}, u32[]{:S(2)}) collective-permute-start(bf16[128,512]{1,0:T(8,128)(2,1)S(1)} %convolution_convert_fusion.1), channel_id=1, source_target_pairs={{0,3},{1,4},{2,5},{3,6},{4,7},{5,8},{6,9},{7,10},{8,11},{9,12},{10... | collective-permute-start | bytes 393224 | tf_op jit(solution)/shard_map/ppermute | solution.py:18
  267.3 6.8 %collective-permute-start.6 = (bf16[128,512]{1,0:T(8,128)(2,1)S(1)}, bf16[128,512]{1,0:T(8,128)(2,1)S(1)}, u32[]{:S(2)}, u32[]{:S(2)}) collective-permute-start(bf16[128,512]{1,0:T(8,128)(2,1)S(1)} %convolution_convert_fusion.1), channel_id=1, source_target_pairs={{0,2},{1,3},{2,4},{3,5},{4,6},{5,7},{6,8},{7,9},{8,10},{9,11},{10,... | collective-permute-start | bytes 393224 | tf_op jit(solution)/shard_map/ppermute | solution.py:18
  269.6 4.6 %collective-permute-start.7 = (bf16[128,512]{1,0:T(8,128)(2,1)S(1)}, bf16[128,512]{1,0:T(8,128)(2,1)S(1)}, u32[]{:S(2)}, u32[]{:S(2)}) collective-permute-start(bf16[128,512]{1,0:T(8,128)(2,1)S(1)} %convolution_convert_fusion.1), channel_id=1, source_target_pairs={{0,1},{1,2},{2,3},{3,4},{4,5},{5,6},{6,7},{7,8},{8,9},{9,10},{10,1... | collective-permute-start | bytes 393224 | tf_op jit(solution)/shard_map/ppermute | solution.py:18
  288.6 9.4 %copy-start.6 = (bf16[1024,256]{0,1:T(8,128)(2,1)S(1)}, bf16[1024,256]{0,1:T(8,128)(2,1)}, u32[]{:S(2)}) copy-start(bf16[1024,256]{0,1:T(8,128)(2,1)} %copy.40) | copy-start | bytes 1572868
where the time goes:
time: 315 us; the launch traced here: 309 us
  blocking collectives  74.9 us (24%)
  local copies, waits for them, and re-layouts  60 us (19%)
  matrix products  57.4 us (18%)
  waiting for transfers between devices  43.3 us (14%)
  starting transfers between devices  42.6 us (14%)
  other arithmetic  29.3 us (9%)
    all_to_all x1, blocking collectives, on_device(): lax.all_to_all(copies, 'seq', split_axis=0, concat_axis=0, tiled=True)  74.9 us
    all_to_all x1, waiting for transfers between devices, on_device(): lax.all_to_all(partial_value, 'seq', split_axis=0, concat_axis=0, tiled=T...  43.3 us
    ppermute x8, starting transfers between devices, from_behind(): return lax.ppermute(block, axis, route)  37.8 us
    dot_general x1, matrix products, on_device(): jnp.dot(hidden, down_proj, preferred_element_type=jnp.float32)  26.3 us
    unnamed x38, local copies, waits for them, and re-layouts  21.7 us
    dot_general x2, matrix products, attend(): jnp.einsum('qkgd,skd->kgqs', query_heads, key_heads, preferred_element_ty...  11.1 us
    dot_general x2, matrix products, attend(): jnp.einsum('kgqs,skd->qkgd', weights.astype(jnp.bfloat16), value_heads, p...  10.4 us
    reduce_sum x2, other arithmetic, attend(): totals = jnp.sum(weights, axis=-1)  10.3 us
  transfers between devices with their start and end apart: 9, of which 1 were waited for; matrix products, arithmetic and copies ran while one was open for 6% of the time, Pallas kernels for 0%

commit v1 on v0

v1 whole, which is shorter than its diff:
```python
import functools

import jax
import jax.numpy as jnp
from jax import lax
from jax.experimental import pallas as pl
from jax.experimental.pallas import tpu as pltpu
from jax.sharding import PartitionSpec as P

HEADS = 32
KV_HEADS = 4
HEAD_DIM = 64
EXPERTS = 16
TOP = 4
WINDOW = 128
STRETCH = 1024
EPS = 1e-05
MASKED = -1e30
NT = (((1,), (1,)), ((), ()))


def dot(a, b, dims=(((1,), (0,)), ((), ()))):
    return lax.dot_general(a, b, dims, preferred_element_type=jnp.float32)


def transposed(block):
    rows = block.shape[0]
    edges = list(range(0, rows, 128)) + [rows]
    parts = [block[a:b, :].T for a, b in zip(edges[:-1], edges[1:])]
    return jnp.concatenate(parts, axis=1)


def slots(routes, capacity):
    tokens = routes.shape[1]
    expert = lax.broadcasted_iota(jnp.int32, (EXPERTS, tokens), 0)
    named = jnp.zeros((EXPERTS, tokens), jnp.float32)
    for k in range(TOP):
        named = named + (routes[k : k + 1, :] == expert).astype(jnp.float32)
    before = lax.broadcasted_iota(jnp.int32, (tokens, tokens), 0)
    after = lax.broadcasted_iota(jnp.int32, (tokens, tokens), 1)
    ahead = (before < after).astype(jnp.bfloat16)
    rank = dot(named.astype(jnp.bfloat16), ahead).astype(jnp.int32)
    rank = jnp.where(named > 0.5, rank, -1)
    place = lax.broadcasted_iota(jnp.int32, (EXPERTS, capacity, tokens), 1)
    return (rank[:, None, :] == place).astype(jnp.float32)


def prep_kernel(routes_ref, stream_ref, gain_ref, out_ref):
    capacity = out_ref.shape[1]
    stream = stream_ref[...].astype(jnp.float32)
    second = jnp.sum(stream * stream, axis=0, keepdims=True) / stream.shape[0]
    scaled = stream * lax.rsqrt(second + EPS)
    tokens = (transposed(scaled) * gain_ref[...]).astype(jnp.bfloat16)
    chosen = slots(routes_ref[...], capacity)
    chosen = chosen.reshape(EXPERTS * capacity, -1).astype(jnp.bfloat16)
    rows = dot(chosen, tokens).astype(jnp.bfloat16)
    out_ref[...] = rows.reshape(out_ref.shape)


def prep(routes, stream, gain):
    rows, width = stream.shape
    capacity = rows * TOP // EXPERTS
    return pl.pallas_call(
        prep_kernel,
        out_shape=jax.ShapeDtypeStruct((EXPERTS, capacity, width), jnp.bfloat16),
        cost_estimate=pl.CostEstimate(
            flops=2 * rows * TOP * rows * width, bytes_accessed=12 * rows * width, transcendentals=0
        ),
        name="prep",
    )(routes.T, stream.T, gain.reshape(1, -1))


def experts_kernel(x_ref, gate_ref, up_ref, down_ref, out_ref, acc_ref):
    step = pl.program_id(1)
    rows = x_ref[...]
    gate = dot(rows, gate_ref[...], NT)
    up = dot(rows, up_ref[...], NT)
    hidden = (jax.nn.silu(gate) * up).astype(jnp.bfloat16)
    part = dot(hidden, down_ref[...])

    @pl.when(step == 0)
    def _():
        acc_ref[...] = part

    @pl.when(step > 0)
    def _():
        acc_ref[...] += part

    @pl.when(step == pl.num_programs(1) - 1)
    def _():
        out_ref[...] = acc_ref[...].astype(jnp.bfloat16)


def tile_of(extent, most, unit):
    for size in range(min(extent, most), 0, -1):
        if extent % size == 0 and (size % unit == 0 or size == extent):
            return size
    return extent


def experts(rows, gate_proj, up_proj, down_proj):
    count, width = rows.shape
    hidden = down_proj.shape[0]
    tile = tile_of(hidden, 480, 16)
    block = tile_of(count, 512, 16)
    return pl.pallas_call(
        experts_kernel,
        grid=(count // block, hidden // tile),
        in_specs=[
            pl.BlockSpec((block, width), lambda i, j: (i, 0)),
            pl.BlockSpec((tile, width), lambda i, j: (j, 0)),
            pl.BlockSpec((tile, width), lambda i, j: (j, 0)),
            pl.BlockSpec((tile, width), lambda i, j: (j, 0)),
        ],
        out_specs=pl.BlockSpec((block, width), lambda i, j: (i, 0)),
        out_shape=jax.ShapeDtypeStruct((count, width), jnp.bfloat16),
        scratch_shapes=[pltpu.VMEM((block, width), jnp.float32)],
        cost_estimate=pl.CostEstimate(
            flops=6 * count * width * hidden,
            bytes_accessed=6 * width * hidden + 4 * count * width,
            transcendentals=count * hidden,
        ),
        name="experts",
    )(rows, gate_proj.T, up_proj.T, down_proj)


def combine_kernel(
    routes_ref, gates_ref, returned_ref, stream_ref, gain_ref, proj_ref, next_ref, kv_ref
):
    splits, capacity = returned_ref.shape[1:3]
    width = returned_ref.shape[3]
    routes = routes_ref[...]
    tokens = routes.shape[1]
    expert = lax.broadcasted_iota(jnp.int32, (EXPERTS, tokens), 0)
    gate = jnp.zeros((EXPERTS, tokens), jnp.float32)
    for k in range(TOP):
        gate = gate + jnp.where(routes[k : k + 1, :] == expert, gates_ref[k : k + 1, :], 0.0)
    chosen = slots(routes, capacity) * gate[:, None, :]
    if splits > 1:
        chosen = jnp.broadcast_to(
            chosen[:, None], (EXPERTS, splits, capacity, tokens)
        )
    mix = transposed(chosen.reshape(EXPERTS * splits * capacity, tokens))
    high = mix.astype(jnp.bfloat16)
    rest = mix - high.astype(jnp.float32)
    middle = rest.astype(jnp.bfloat16)
    low = (rest - middle.astype(jnp.float32)).astype(jnp.bfloat16)
    parts = jnp.concatenate([high, middle, low], axis=0)
    summed = dot(parts, returned_ref[...].reshape(-1, width))
    summed = summed[:tokens] + (summed[tokens : 2 * tokens] + summed[2 * tokens :])
    stream = transposed(stream_ref[...].astype(jnp.float32))
    following = (stream + summed).astype(jnp.bfloat16)
    widened = following.astype(jnp.float32)
    for a in range(0, width, 128):
        b = min(a + 128, width)
        next_ref[a:b, :] = widened[:, a:b].T.astype(jnp.bfloat16)
    second = jnp.sum(widened * widened, axis=1, keepdims=True) / width
    attn_input = (widened * lax.rsqrt(second + EPS) * gain_ref[...]).astype(jnp.bfloat16)
    kv_ref[...] = dot(attn_input, proj_ref[...]).astype(jnp.bfloat16)


def combine(routes, gates, returned, stream, gain, kv_proj):
    rows, width = stream.shape
    following, kv = pl.pallas_call(
        combine_kernel,
        out_shape=(
            jax.ShapeDtypeStruct((width, rows), jnp.bfloat16),
            jax.ShapeDtypeStruct((rows, kv_proj.shape[1]), jnp.bfloat16),
        ),
        cost_estimate=pl.CostEstimate(
            flops=6 * rows * TOP * rows * width,
            bytes_accessed=2 * returned.size + 4 * rows * width + 2 * kv_proj.size,
            transcendentals=0,
        ),
        name="combine",
    )(routes.T, gates.T, returned, stream.T, gain.reshape(1, -1), kv_proj)
    return following.T, kv


def spread(block, left):
    empty = jnp.zeros_like(block)
    return jnp.concatenate([block, empty] if left else [empty, block], axis=1)


def attend_kernel(mask_fn, *refs):
    scalar_ref, query_ref, own_ref = refs[:3]
    other_refs, out_ref = refs[3:-1], refs[-1]
    rows = query_ref.shape[0]
    half = own_ref.shape[1] // 2
    pairs = query_ref.shape[1] // (2 * HEAD_DIM)
    per_kv = pairs // KV_HEADS
    shared = sum(ref.shape[0] for ref in other_refs)
    own_mask, other_mask = mask_fn(scalar_ref, rows, shared)
    own_mask = jnp.concatenate([own_mask] * per_kv, axis=0)
    if other_mask.shape[0] > 1:
        other_mask = jnp.concatenate([other_mask] * per_kv, axis=0)
    lane = lax.broadcasted_iota(jnp.int32, (per_kv * rows, 2 * HEAD_DIM), 1)
    for g in range(KV_HEADS):
        cols = slice(g * HEAD_DIM, (g + 1) * HEAD_DIM)
        vcols = slice(half + g * HEAD_DIM, half + (g + 1) * HEAD_DIM)
        queries = jnp.concatenate(
            [
                query_ref[:, (g * per_kv + p) * 2 * HEAD_DIM : (g * per_kv + p + 1) * 2 * HEAD_DIM]
                for p in range(per_kv)
            ],
            axis=0,
        )
        own_keys = own_ref[:, cols] * jnp.bfloat16(0.125)
        other_keys = jnp.concatenate([ref[:, cols] for ref in other_refs], axis=0)
        other_keys = other_keys * jnp.bfloat16(0.125)
        own_values = own_ref[:, vcols]
        other_values = jnp.concatenate([ref[:, vcols] for ref in other_refs], axis=0)
        mixed, totals = [], []
        for left in (True, False):
            own = dot(queries, spread(own_keys, left), NT)
            other = dot(queries, spread(other_keys, left), NT)
            own = jnp.where(own_mask, own, MASKED)
            other = jnp.where(other_mask, other, MASKED)
            peak = jnp.maximum(
                jnp.max(own, axis=1, keepdims=True), jnp.max(other, axis=1, keepdims=True)
            )
            own = jnp.exp(own - peak)
            other = jnp.exp(other - peak)
            totals.append(
                jnp.sum(own, axis=1, keepdims=True) + jnp.sum(other, axis=1, keepdims=True)
            )
            mixed.append(
                dot(own.astype(jnp.bfloat16), spread(own_values, left))
                + dot(other.astype(jnp.bfloat16), spread(other_values, left))
            )
        total = jnp.where(lane < HEAD_DIM, totals[0], totals[1])
        result = ((mixed[0] + mixed[1]) / total).astype(jnp.bfloat16)
        for p in range(per_kv):
            at = (g * per_kv + p) * 2 * HEAD_DIM
            out_ref[:, at : at + 2 * HEAD_DIM] = result[p * rows : (p + 1) * rows]


def attend(mask_fn, scalar, queries, own, others, name):
    rows, width = queries.shape
    keys = rows + sum(other.shape[0] for other in others)
    vmem = pl.BlockSpec(memory_space=pltpu.VMEM)
    return pl.pallas_call(
        functools.partial(attend_kernel, mask_fn),
        in_specs=[pl.BlockSpec(memory_space=pltpu.SMEM)] + [vmem] * (2 + len(others)),
        out_specs=vmem,
        out_shape=jax.ShapeDtypeStruct((rows, width), jnp.bfloat16),
        cost_estimate=pl.CostEstimate(
            flops=8 * rows * width * keys,
            bytes_accessed=4 * rows * width + 4 * keys * own.shape[1],
            transcendentals=rows * HEADS * keys,
        ),
        name=name,
    )(scalar, queries, own, *others)


def window_masks(scalar_ref, rows, shared):
    device = scalar_ref[0]
    token = lax.broadcasted_iota(jnp.int32, (rows, rows), 0)
    key = lax.broadcasted_iota(jnp.int32, (rows, rows), 1)
    own = (key <= token) & (token - key < WINDOW)
    token = lax.broadcasted_iota(jnp.int32, (rows, shared), 0)
    key = lax.broadcasted_iota(jnp.int32, (rows, shared), 1) - shared
    return own, (token - key < WINDOW) & (key + device * rows >= 0)


def tract_masks(scalar_ref, rows, shared):
    token = lax.broadcasted_iota(jnp.int32, (rows, rows), 0)
    key = lax.broadcasted_iota(jnp.int32, (rows, rows), 1)
    block = lax.broadcasted_iota(jnp.int32, (1, shared), 1) // rows
    valid = jnp.zeros((1, shared), jnp.int32)
    for b in range(shared // rows):
        valid = jnp.where(block == b, scalar_ref[b], valid)
    return key <= token, valid > 0


def exchange(own, device, devices, per_half):
    everyone = range(devices)
    odd = lambda i: (i // per_half) % 2 == 1
    route = [(i, i + per_half) for i in everyone if odd(i) and i + per_half < devices]
    before = lax.ppermute(own, "seq", route)
    held, sources = [before], [("before", 0)]
    group = (device // per_half) % 2
    has_before = ((group == 0) & (device >= per_half)).astype(jnp.int32)
    parts = [(own, before)]
    pack = jnp.concatenate([own, before], axis=0)
    others = [before]
    flags = [has_before]
    masks = [0]
    step = per_half // 2
    while step:
        came = lax.ppermute(pack, "seq", [(i, i ^ step) for i in everyone])
        others.append(came)
        for m in masks:
            flags.append(((device ^ (m ^ step)) < device).astype(jnp.int32))
            flags.append(has_before)
        masks = masks + [m ^ step for m in masks]
        pack = jnp.concatenate([pack, came], axis=0)
        step //= 2
    return others, jnp.stack(flags)


def on_device(
    window_queries,
    window_kv,
    stream,
    moe_gain,
    routes,
    route_gates,
    gate_proj,
    up_proj,
    down_proj,
    attn_gain,
    kv_proj,
    tract_queries,
):
    rows_here, model_width = stream.shape
    device = lax.axis_index("seq")
    devices = lax.axis_size("seq")
    capacity = rows_here * TOP // EXPERTS
    split_count = devices // EXPERTS
    rim = lax.ppermute(window_kv, "seq", [(i - 1, i) for i in range(1, devices)])
    outgoing = prep(routes, stream, moe_gain)
    copies = jnp.repeat(outgoing, split_count, axis=0) if split_count > 1 else outgoing
    arrived = lax.all_to_all(copies, "seq", split_axis=0, concat_axis=0, tiled=True)
    block_out = experts(arrived.reshape(-1, model_width), gate_proj, up_proj, down_proj)
    returned = lax.all_to_all(
        block_out.reshape(arrived.shape), "seq", split_axis=0, concat_axis=0, tiled=True
    )
    attn_window = attend(
        window_masks, device.reshape(1).astype(jnp.int32), window_queries, window_kv, [rim], "window"
    )
    returned = returned.reshape(EXPERTS, split_count, capacity, model_width)
    stream_next, tract_kv = combine(routes, route_gates, returned, stream, attn_gain, kv_proj)
    per_half = STRETCH // 2 // rows_here
    others, flags = exchange(tract_kv, device, devices, per_half)
    attn_tract = attend(tract_masks, flags, tract_queries, tract_kv, others, "tract")
    return (attn_window, stream_next, attn_tract)


def solution(mesh):
    return jax.shard_map(
        on_device,
        mesh=mesh,
        in_specs=(
            P(("groups", "seq"), None),
            P(("groups", "seq"), None),
            P(("groups", "seq"), None),
            P(),
            P(("groups", "seq"), None),
            P(("groups", "seq"), None),
            P(None, "seq"),
            P(None, "seq"),
            P("seq", None),
            P(),
            P(),
            P(("groups", "seq"), None),
        ),
        out_specs=(
            P(("groups", "seq"), None),
            P(("groups", "seq"), None),
            P(("groups", "seq"), None),
        ),
        check_vma=False,
    )
```

time: 315 us -> 224 us (0.71)
  the two profiles are of different devices: /device:TPU:0 before, /device:TPU:16 now
where the time goes in v1:
time: 224 us; the launch traced here: 223 us
  waiting for transfers between devices  82.9 us (37%)
  blocking collectives  73.5 us (33%)
  Pallas kernels  49.3 us (22%)
  starting transfers between devices  8.95 us (4%)
  local copies, waits for them, and re-layouts  5.1 us (2%)
  other arithmetic  2.58 us (1%)
    all_to_all x1, blocking collectives, on_device(): lax.all_to_all(copies, 'seq', split_axis=0, concat_axis=0, tiled=True)  73.5 us
    all_to_all x1, waiting for transfers between devices, on_device(): lax.all_to_all(block_out.reshape(arrived.shape), 'seq', split_axis=0, con...  66.7 us
    pallas_call x1, Pallas kernels, experts(): pl.pallas_call(experts_kernel, grid=(count // block, hidden // tile), in_...  23.9 us
    pallas_call x2, Pallas kernels, attend(): pl.pallas_call(functools.partial(attend_kernel, mask_fn), in_specs=[pl.Bl...  15.1 us
    ppermute x2, waiting for transfers between devices, exchange(): came = lax.ppermute(pack, 'seq', [(i, i ^ step) for i in everyone])  6.58 us
    pallas_call x1, Pallas kernels, combine(): pl.pallas_call(combine_kernel, out_shape=(jax.ShapeDtypeStruct((width, ro...  6.11 us
    ppermute x1, waiting for transfers between devices, exchange(): before = lax.ppermute(own, 'seq', route)  5.77 us
    all_to_all x1, starting transfers between devices, on_device(): lax.all_to_all(block_out.reshape(arrived.shape), 'seq', split_axis=0, con...  4.94 us
  transfers between devices with their start and end apart: 5, of which 4 were waited for; matrix products, arithmetic and copies ran while one was open for 1% of the time, Pallas kernels for 2%

profile of v1, /device:TPU:16, one launch (start us, length us, event | category | flops | bytes accessed | tf_op | source)
XLA Modules:
  0.0 223.1 jit_solution(17649971392057519297)
XLA Ops:
  0.6 1.3 reshape.25.gain_ref
  1.9 4.2 %prep.1 = bf16[16,32,2880]{2,1,0:T(8,128)(2,1)} custom-call(s32[4,128]{1,0:T(4,128)} %bitcast.19, bf16[2880,128]{1,0:T(8,128)(2,1)} %bitcast.17, f32[1,2880]{1,0:T(1,128)} %reshape.25.gain_ref), custom_call_target="tpu_custom_call" | custom-call | flops 377487360 | bytes 4423680 | tf_op jit(solution)/shard_map/prep/pallas_call | solution.py:63
  6.1 73.5 %all_to_all.10 = bf16[16,32,2880]{2,1,0:T(8,128)(2,1)} all-to-all(bf16[16,32,2880]{2,1,0:T(8,128)(2,1)} %prep.1), channel_id=1, replica_groups=mesh['groups'=2,'seq'=16] {'seq'}, dimensions={0} | all-to-all | bytes 5898240 | tf_op jit(solution)/shard_map/all_to_all | solution.py:324
  79.6 23.9 %experts.1 = bf16[512,2880]{1,0:T(8,128)(2,1)} custom-call(bf16[512,2880]{1,0:T(8,128)(2,1)} %bitcast.16, bf16[1440,2880]{1,0:T(8,128)(2,1)} %bitcast.22, bf16[1440,2880]{1,0:T(8,128)(2,1)} %bitcast.23, bf16[1440,2880]{1,0:T(8,128)(2,1)} %down_ref.1), custom_call_target="tpu_custom_call" | custom-call | flops 12740198400 | bytes 30781440 | tf_op jit(solution)/shard_map/experts/pallas_call | solution.py:106
  103.6 4.9 %all-to-all-start.1 = ((bf16[16,32,2880]{2,1,0:T(8,128)(2,1)}), bf16[16,32,2880]{2,1,0:T(8,128)(2,1)S(1)}, u32[]{:S(2)}, u32[]{:S(2)}) async-start(bf16[16,32,2880]{2,1,0:T(8,128)(2,1)} %bitcast.15), calls=%async_computation.1 | async-start | bytes 6029312 | tf_op jit(solution)/shard_map/all_to_all | solution.py:326
  108.5 0.6 reshape.29.gain_ref
  109.1 66.7 %all-to-all-done.1 = bf16[16,32,2880]{2,1,0:T(8,128)(2,1)S(1)} async-done(((bf16[16,32,2880]{2,1,0:T(8,128)(2,1)}), bf16[16,32,2880]{2,1,0:T(8,128)(2,1)S(1)}, u32[]{:S(2)}, u32[]{:S(2)}) %all-to-all-start.1) | async-done | bytes 2949152 | tf_op jit(solution)/shard_map/all_to_all | solution.py:326
  175.8 1.6 copy-done
  177.4 6.1 %combine.1 = (bf16[2880,128]{1,0:T(8,128)(2,1)}, bf16[128,512]{1,0:T(8,128)(2,1)}) custom-call(s32[4,128]{1,0:T(4,128)} %bitcast.20, f32[4,128]{1,0:T(4,128)} %bitcast.21, bf16[16,1,32,2880]{3,2,1,0:T(8,128)(2,1)} %bitcast.14, bf16[2880,128]{1,0:T(8,128)(2,1)} %bitcast.18, f32[1,2880]{1,0:T(1,128)} %reshape.29.gain_ref, bf16[2880,512]{1,0:T(8,128)(2,1)} %proj_ref.1), custom_call_target="tpu_custom_call" | custom-call | flops 1132462080 | bytes 7372800 | tf_op jit(solution)/shard_map/combine/pallas_call | solution.py:164
  183.5 1.3 collective-permute-start.1
  184.8 5.8 %collective-permute-done.1.refs_3_ = bf16[128,512]{1,0:T(8,128)(2,1)S(1)} collective-permute-done((bf16[128,512]{1,0:T(8,128)(2,1)}, bf16[128,512]{1,0:T(8,128)(2,1)S(1)}, u32[]{:S(2)}, u32[]{:S(2)}) %collective-permute-start.1) | collective-permute-done | bytes 131104 | tf_op jit(solution)/shard_map/ppermute | solution.py:280
  190.6 1.0 pad_maximum_fusion.1
  191.5 0.1 collective-permute-start.2
  191.6 6.6 %collective-permute-done.2.refs_4_ = bf16[256,512]{1,0:T(8,128)(2,1)S(1)} collective-permute-done((bf16[256,512]{1,0:T(8,128)(2,1)S(1)}, bf16[256,512]{1,0:T(8,128)(2,1)S(1)}, u32[]{:S(2)}, u32[]{:S(2)}) %collective-permute-start.2) | collective-permute-done | bytes 262176 | tf_op jit(solution)/shard_map/ppermute | solution.py:291
  198.2 1.0 pad_maximum_fusion
  199.2 0.1 collective-permute-start.3
  199.3 2.6 %collective-permute-start = (bf16[128,512]{1,0:T(8,128)(2,1)S(1)}, bf16[128,512]{1,0:T(8,128)(2,1)S(1)}, u32[]{:S(2)}, u32[]{:S(2)}) collective-permute-start(bf16[128,512]{1,0:T(8,128)(2,1)S(1)} %copy-done.5), channel_id=1, source_target_pairs={{0,1},{1,2},{2,3},{3,4},{4,5},{5,6},{6,7},{7,8},{8,9},{9,10},{10,1... | collective-permute-start | bytes 393224 | tf_op jit(solution)/shard_map/ppermute | solution.py:321
  201.9 0.1 stack.28
  202.1 0.6 stack.29.refs_0_
  202.6 3.9 %collective-permute-done.refs_3_ = bf16[128,512]{1,0:T(8,128)(2,1)S(1)} collective-permute-done((bf16[128,512]{1,0:T(8,128)(2,1)S(1)}, bf16[128,512]{1,0:T(8,128)(2,1)S(1)}, u32[]{:S(2)}, u32[]{:S(2)}) %collective-permute-start) | collective-permute-done | bytes 131104 | tf_op jit(solution)/shard_map/ppermute | solution.py:321
  206.5 0.7 copy-done.6
  207.2 5.3 %window.1 = bf16[128,2048]{1,0:T(8,128)(2,1)} custom-call(s32[1]{0:T(128)} %bitcast.refs_0_, bf16[128,2048]{1,0:T(8,128)(2,1)} %refs_1_.2, bf16[128,512]{1,0:T(8,128)(2,1)} %refs_2_.1, bf16[128,512]{1,0:T(8,128)(2,1)} %copy-done.6), custom_call_target="tpu_custom_call" | custom-call | flops 536870912 | bytes 1572864 | tf_op jit(solution)/shard_map/window/pallas_call | solution.py:242
  212.5 0.8 copy-done.4
  213.3 9.8 %tract.1 = bf16[128,2048]{1,0:T(8,128)(2,1)} custom-call(s32[7]{0:T(128)} %stack.29.refs_0_, bf16[128,2048]{1,0:T(8,128)(2,1)} %refs_1_.3, bf16[128,512]{1,0:T(8,128)(2,1)} %get-tuple-element.6.refs_2_, bf16[128,512]{1,0:T(8,128)(2,1)} %copy-done.1, bf16[256,512]{1,0:T(8,128)(2,1)} %copy-done.2, bf16[512,512]{1,0:T(8,128)(2,1)} %copy-done.4), custom_call_target="tpu_custom_call" | custom-call | flops 2147483648 | bytes 3145728 | tf_op jit(solution)/shard_map/tract/pallas_call | solution.py:242
  (12 shorter events, 0.0 us)
Async XLA Ops:
  103.6 4.9 %copy-start.3 = (f32[2880]{0:T(1024)S(1)}, f32[2880]{0:T(1024)}, u32[]{:S(2)}) copy-start(f32[2880]{0:T(1024)} %param.21) | copy-start | bytes 34564
  103.6 72.2 %all-to-all-start.1 = ((bf16[16,32,2880]{2,1,0:T(8,128)(2,1)}), bf16[16,32,2880]{2,1,0:T(8,128)(2,1)S(1)}, u32[]{:S(2)}, u32[]{:S(2)}) async-start(bf16[16,32,2880]{2,1,0:T(8,128)(2,1)} %bitcast.15), calls=%async_computation.1 | async-start | bytes 6029312 | tf_op jit(solution)/shard_map/all_to_all | solution.py:326
  175.8 1.6 copy-start
  177.4 21.9 %copy-start.5 = (bf16[128,512]{1,0:T(8,128)(2,1)S(1)}, bf16[128,512]{1,0:T(8,128)(2,1)}, u32[]{:S(2)}) copy-start(bf16[128,512]{1,0:T(8,128)(2,1)} %refs_2_.1) | copy-start | bytes 393220
  183.5 7.1 %collective-permute-start.1 = (bf16[128,512]{1,0:T(8,128)(2,1)}, bf16[128,512]{1,0:T(8,128)(2,1)S(1)}, u32[]{:S(2)}, u32[]{:S(2)}) collective-permute-start(bf16[128,512]{1,0:T(8,128)(2,1)} %get-tuple-element.6.refs_2_), channel_id=1, source_target_pairs={{4,8},{5,9},{6,10},{7,11},{20,24},{21,25},{22,26},{23,27}} | collective-permute-start | bytes 393224 | tf_op jit(solution)/shard_map/ppermute | solution.py:280
  190.6 21.9 %copy-start.1 = (bf16[128,512]{1,0:T(8,128)(2,1)}, bf16[128,512]{1,0:T(8,128)(2,1)S(1)}, u32[]{:S(2)}) copy-start(bf16[128,512]{1,0:T(8,128)(2,1)S(1)} %collective-permute-done.1.refs_3_) | copy-start | bytes 393220
  191.5 6.7 %collective-permute-start.2 = (bf16[256,512]{1,0:T(8,128)(2,1)S(1)}, bf16[256,512]{1,0:T(8,128)(2,1)S(1)}, u32[]{:S(2)}, u32[]{:S(2)}) collective-permute-start(bf16[256,512]{1,0:T(8,128)(2,1)S(1)} %pad_maximum_fusion.1), channel_id=1, source_target_pairs={{0,2},{1,3},{2,0},{3,1},{4,6},{5,7},{6,4},{7,5},{8,10},{9,11},{10,... | collective-permute-start | bytes 786440 | tf_op jit(solution)/shard_map/ppermute | solution.py:291
  198.2 14.3 %copy-start.2 = (bf16[256,512]{1,0:T(8,128)(2,1)}, bf16[256,512]{1,0:T(8,128)(2,1)S(1)}, u32[]{:S(2)}) copy-start(bf16[256,512]{1,0:T(8,128)(2,1)S(1)} %collective-permute-done.2.refs_4_) | copy-start | bytes 786436
  199.2 13.2 %collective-permute-start.3 = (bf16[512,512]{1,0:T(8,128)(2,1)S(1)}, bf16[512,512]{1,0:T(8,128)(2,1)S(1)}, u32[]{:S(2)}, u32[]{:S(2)}) collective-permute-start(bf16[512,512]{1,0:T(8,128)(2,1)S(1)} %pad_maximum_fusion), channel_id=1, source_target_pairs={{0,1},{1,0},{2,3},{3,2},{4,5},{5,4},{6,7},{7,6},{8,9},{9,8},{10,11... | collective-permute-start | bytes 1572872 | tf_op jit(solution)/shard_map/ppermute | solution.py:291
  199.3 7.2 %collective-permute-start = (bf16[128,512]{1,0:T(8,128)(2,1)S(1)}, bf16[128,512]{1,0:T(8,128)(2,1)S(1)}, u32[]{:S(2)}, u32[]{:S(2)}) collective-permute-start(bf16[128,512]{1,0:T(8,128)(2,1)S(1)} %copy-done.5), channel_id=1, source_target_pairs={{0,1},{1,2},{2,3},{3,4},{4,5},{5,6},{6,7},{7,8},{8,9},{9,10},{10,1... | collective-permute-start | bytes 393224 | tf_op jit(solution)/shard_map/ppermute | solution.py:321
  206.5 0.7 copy-start.6
  212.5 0.8 copy-start.4
